TPU v7x, 32 devices: a whole 2x2x4 slice. The times are simulated.
32 devices in a mesh: leaf: 2 (over core), row: 4 (over y, x), col: 4 (over z).
Axes of the slice: x: 2, y: 2, z: 4, core: 2. Of those that a mesh axis runs over, the one named last changes fastest.
Arguments:
- sketch_leaf: bfloat16 [16384, 256], P(('leaf', 'row'), 'col'), may hold values from -6 to 6
- sketch_sep: bfloat16 [8192, 256], P(('row', 'col')), may hold values from -6 to 6
- leaf_inverse: bfloat16 [16384, 8192], P(('leaf', 'col'), 'row'), as said below
- coupling: bfloat16 [16384, 2048], P(('leaf', 'col'), 'row'), may hold values from -0.0625 to 0.0625
- sep_inverse: bfloat16 [8192, 8192], P('leaf', ('row', 'col'))
- front_map: int32 [2, 16], replicated, may hold values from 0 to 63, as said below
Outputs:
- sketch_out_leaf: float32 [16384, 256], P(('leaf', 'row'), 'col')
- sketch_out_sep: float32 [8192, 256], P(('row', 'col'))
Inputs may be any that keep to these rules, and one draw needn't show every extreme that they name: `front_map`: row block q of every section's coupling lies in separator blocks q * 4 to q * 4 + 3. leaf_inverse and sep_inverse are inverses of lower triangular factor blocks (in natural order), stored in block-cyclic order.
All inputs are finite; a program needn't handle non-finite values.
Results may differ from a plain program's by a relative error of at most 0.024.
Values may be sent and summed in bfloat16 or wider, within the bound.
No kernel may reach another device: no remote copies, remote signals or barrier semaphores. Data moves between devices by JAX's collectives and lax.ppermute only.
A program may use at most 64 MiB of HBM per device.

v0:
```python
import jax
import jax.numpy as jnp
from jax import lax
from jax.sharding import PartitionSpec as P


def contract_rows(left, right):
    return lax.dot_general(
        left, right, (((0,), (0,)), ((), ())), preferred_element_type=jnp.float32
    )


def shards(sketch_leaf, sketch_sep, leaf_inverse, coupling, sep_inverse, front_map):
    columns = sketch_leaf.shape[1] * lax.axis_size("col")
    q_index = lax.axis_index("row") * lax.axis_size("col") + lax.axis_index("col")
    section = lax.axis_index("leaf")
    partial_value = jnp.dot(
        leaf_inverse,
        lax.all_gather(sketch_leaf, "col", axis=1, tiled=True),
        preferred_element_type=jnp.float32,
    )
    front_z = lax.psum_scatter(partial_value, "row", scatter_dimension=1, tiled=True).astype(
        jnp.bfloat16
    )
    coupled_part = contract_rows(coupling, lax.all_gather(front_z, "row", axis=1, tiled=True))
    coupled = lax.psum_scatter(coupled_part, "col", scatter_dimension=0, tiled=True).astype(
        jnp.bfloat16
    )
    block_rows = coupled.shape[0]
    group = sketch_sep.shape[0] // block_rows
    own_slot = front_map[section, q_index] - q_index * group
    blocks = lax.all_gather(coupled, "leaf", axis=0, tiled=True)
    slots = front_map[:, q_index] - q_index * group
    place = (slots[:, None] == jnp.arange(group, dtype=jnp.int32)[None, :]).astype(jnp.bfloat16)
    stacked = blocks.reshape(slots.shape[0], block_rows, columns)
    total = jnp.einsum("sg,sik->gik", place, stacked, preferred_element_type=jnp.float32).reshape(
        group * block_rows, columns
    )
    sep_rhs = (sketch_sep.astype(jnp.float32) - total).astype(jnp.bfloat16)
    sep_part = jnp.dot(sep_inverse, sep_rhs, preferred_element_type=jnp.float32)
    sep_mid = lax.psum(sep_part.astype(jnp.bfloat16), ("row", "col"))
    sketch_out_sep = lax.psum(
        contract_rows(sep_inverse, sep_mid).astype(jnp.bfloat16), "leaf"
    ).astype(jnp.float32)
    sep_round = sketch_out_sep.astype(jnp.bfloat16)
    pulled = lax.dynamic_slice_in_dim(sep_round, own_slot * block_rows, block_rows, 0)
    back_part = jnp.dot(
        coupling,
        lax.all_gather(pulled, "col", axis=0, tiled=True),
        preferred_element_type=jnp.float32,
    )
    back_slice = lax.psum_scatter(
        back_part.astype(jnp.bfloat16), "row", scatter_dimension=1, tiled=True
    ).astype(jnp.float32)
    leaf_rhs = (front_z.astype(jnp.float32) - back_slice).astype(jnp.bfloat16)
    out_part = contract_rows(leaf_inverse, lax.all_gather(leaf_rhs, "row", axis=1, tiled=True))
    sketch_out_leaf = lax.psum_scatter(
        out_part.astype(jnp.bfloat16), "col", scatter_dimension=1, tiled=True
    ).astype(jnp.float32)
    return (sketch_out_leaf, sketch_out_sep)


def solution(mesh):
    placed = (
        P(("leaf", "row"), "col"),
        P(("row", "col"), None),
        P(("leaf", "col"), "row"),
        P(("leaf", "col"), "row"),
        P("leaf", ("row", "col")),
        P(),
    )
    return jax.shard_map(
        shards,
        mesh=mesh,
        in_specs=placed,
        out_specs=(P(("leaf", "row"), "col"), P(("row", "col"), None)),
        check_vma=False,
    )
```

profile of v0, /device:TPU:0, one launch (start us, length us, event | category | flops | bytes accessed | tf_op | source)
XLA Modules:
  0.0 407.7 jit_solution(16510389504449765819)
XLA Ops:
  7.2 0.0 copy-start
  7.2 0.0 all-gather.4.cloned.1.call-start
  7.2 0.7 all-gather.4.cloned.1.call-update
  7.9 0.0 reduce-scatter.5.cloned.1.call-start
  8.0 32.3 %all-gather.4.cloned.1.call-done = bf16[2048,256]{0,1:T(8,128)(2,1)} async-done(((bf16[2048,64]{0,1:T(8,128)(2,1)}), bf16[2048,256]{0,1:T(8,128)(2,1)}) %all-gather.4.cloned.1.call-update) | async-done | bytes 1048592 | tf_op jit(solution)/shard_map/all_gather | solution.py:19
  40.3 7.3 %fusion.10 = f32[2048,256]{0,1:T(8,128)} fusion(bf16[2048,2048]{1,0:T(8,128)(2,1)} %param.8, bf16[2048,256]{0,1:T(8,128)(2,1)} %all-gather.4.cloned.1.call-done), kind=kOutput, calls=%fused_computation.19 | convolution fusion | flops 2147483648 | bytes 11534336 | tf_op jit(solution)/shard_map/dot_general | solution.py:17
  47.6 0.0 reduce-scatter.5.cloned.1.call-update
  47.6 0.0 all-gather.6.cloned.1.call-start
  47.7 34.7 %reduce-scatter.5.cloned.1.call-done = f32[2048,64]{0,1:T(8,128)} async-done(((f32[2048,256]{0,1:T(8,128)}), f32[2048,64]{0,1:T(8,128)}) %reduce-scatter.5.cloned.1.call-update) | async-done | bytes 524304 | tf_op jit(solution)/shard_map/reduce_scatter | solution.py:22
  82.3 1.8 convert_element_type.53
  84.1 0.0 all-gather.6.cloned.1.call-update
  84.1 0.0 copy-start.4
  84.2 0.0 reduce-scatter.7.cloned.1.call-start
  84.2 27.1 %all-gather.6.cloned.1.call-done = bf16[2048,256]{0,1:T(8,128)(2,1)} async-done(((bf16[2048,64]{0,1:T(8,128)(2,1)}), bf16[2048,256]{0,1:T(8,128)(2,1)}) %all-gather.6.cloned.1.call-update) | async-done | bytes 1048592 | tf_op jit(solution)/shard_map/all_gather | solution.py:25
  111.3 0.0 copy-done
  111.3 2.7 convolution_bitcast_fusion
  114.0 0.0 copy-start.3
  114.0 0.0 reduce-scatter.7.cloned.1.call-update
  114.1 0.0 all-reduce.3.cloned.1.call-start
  114.1 0.0 copy-done.4
  114.1 0.2 subtract_reduce_fusion
  114.3 21.7 %reduce-scatter.7.cloned.1.call-done = f32[128,256]{0,1:T(8,128)} async-done(((f32[512,256]{0,1:T(8,128)}), f32[128,256]{0,1:T(8,128)}) %reduce-scatter.7.cloned.1.call-update) | async-done | bytes 131088 | tf_op jit(solution)/shard_map/reduce_scatter | solution.py:26
  136.0 0.9 convert_element_type.56
  136.9 1.9 all_gather.17
  138.9 0.1 copy.10
  139.0 0.4 fusion.5
  139.5 0.1 copy.11
  139.6 0.0 copy-done.3
  139.6 0.1 fusion.4
  139.7 4.8 %fusion = bf16[4096,256]{0,1:T(8,128)(2,1)} fusion(bf16[512,256]{1,0:T(8,128)(2,1)S(1)} %fusion.4, bf16[4096,512]{1,0:T(8,128)(2,1)} %param.10), kind=kOutput, calls=%fused_computation.1 | convolution fusion | flops 1074790400 | bytes 6553600 | tf_op jit(solution)/shard_map/dot_general | solution.py:40
  144.5 0.0 all-reduce.3.cloned.1.call-update
  144.5 0.0 all-reduce.5.cloned.1.call-start
  144.5 125.0 %all-reduce.3.cloned.1.call-done = bf16[4096,256]{0,1:T(8,128)(2,1)} async-done(((bf16[4096,256]{0,1:T(8,128)(2,1)}), bf16[4096,256]{0,1:T(8,128)(2,1)}) %all-reduce.3.cloned.1.call-update) | async-done | bytes 2097168 | tf_op jit(solution)/shard_map/psum | solution.py:41
  269.5 4.8 %fusion.3 = bf16[512,256]{0,1:T(8,128)(2,1)} fusion(bf16[4096,256]{0,1:T(8,128)(2,1)} %all-reduce.3.cloned.1.call-done, bf16[4096,512]{1,0:T(8,128)(2,1)} %param.10), kind=kOutput, calls=%fused_computation.8 | convolution fusion | flops 1073872896 | bytes 6553600 | tf_op jit(solution)/shard_map/dot_general | solution.py:8
  274.3 0.0 all-reduce.5.cloned.1.call-update
  274.3 0.0 reduce-scatter.9.cloned.1.call-start
  274.4 0.6 dynamic_slice.10
  275.6 16.3 %all-reduce.5.cloned.1.call-done = bf16[512,256]{0,1:T(8,128)(2,1)} async-done(((bf16[512,256]{0,1:T(8,128)(2,1)}), bf16[512,256]{0,1:T(8,128)(2,1)}) %all-reduce.5.cloned.1.call-update) | async-done | bytes 262160 | tf_op jit(solution)/shard_map/psum | solution.py:42
  291.9 0.8 constant_dynamic-slice_fusion
  292.8 13.1 %all_gather.18 = bf16[512,256]{0,1:T(8,128)(2,1)S(1)} all-gather(bf16[128,256]{0,1:T(8,128)(2,1)S(1)} %constant_dynamic-slice_fusion), channel_id=1, replica_groups=mesh['leaf'=2,'row'=4,'col'=4] {'col'}, dimensions={0}, use_global_device_ids=true | all-gather | bytes 327680 | tf_op jit(solution)/shard_map/all_gather | solution.py:49
  305.9 0.0 copy-start.1
  305.9 1.7 fusion.2
  307.6 0.0 reduce-scatter.9.cloned.1.call-update
  307.7 0.0 all-gather.8.cloned.1.call-start
  307.7 28.2 %reduce-scatter.9.cloned.1.call-done = bf16[2048,64]{0,1:T(8,128)(2,1)} async-done(((bf16[2048,256]{0,1:T(8,128)(2,1)}), bf16[2048,64]{0,1:T(8,128)(2,1)}) %reduce-scatter.9.cloned.1.call-update) | async-done | bytes 262160 | tf_op jit(solution)/shard_map/reduce_scatter | solution.py:52
  335.9 0.0 copy-done.1
  335.9 1.7 subtract_convert_fusion
  337.6 0.0 all-gather.8.cloned.1.call-update
  337.6 0.0 copy-start.2
  337.7 0.0 reduce-scatter.11.cloned.1.call-start
  337.7 27.2 %all-gather.8.cloned.1.call-done = bf16[2048,256]{0,1:T(8,128)(2,1)} async-done(((bf16[2048,64]{0,1:T(8,128)(2,1)}), bf16[2048,256]{0,1:T(8,128)(2,1)}) %all-gather.8.cloned.1.call-update) | async-done | bytes 1048592 | tf_op jit(solution)/shard_map/all_gather | solution.py:56
  364.9 7.0 %fusion.1 = bf16[2048,256]{0,1:T(8,128)(2,1)} fusion(bf16[2048,256]{0,1:T(8,128)(2,1)} %all-gather.8.cloned.1.call-done, bf16[2048,2048]{1,0:T(8,128)(2,1)} %param.8), kind=kOutput, calls=%fused_computation.4 | convolution fusion | flops 2148007936 | bytes 10485760 | tf_op jit(solution)/shard_map/dot_general | solution.py:8
  371.9 0.0 reduce-scatter.11.cloned.1.call-update
  371.9 0.0 copy-done.2
  371.9 0.9 copy.12
  372.9 26.5 %reduce-scatter.11.cloned.1.call-done = bf16[2048,64]{0,1:T(8,128)(2,1)} async-done(((bf16[2048,256]{0,1:T(8,128)(2,1)}), bf16[2048,64]{0,1:T(8,128)(2,1)}) %reduce-scatter.11.cloned.1.call-update) | async-done | bytes 262160 | tf_op jit(solution)/shard_map/reduce_scatter | solution.py:57
  399.4 1.8 convert_element_type.68
  (1 shorter events, 0.0 us)
Async XLA Ops:
  7.2 104.1 %copy-start = (bf16[2048,512]{1,0:T(8,128)(2,1)S(1)}, bf16[2048,512]{1,0:T(8,128)(2,1)}, u32[]{:S(2)}) copy-start(bf16[2048,512]{1,0:T(8,128)(2,1)} %param.9) | copy-start | bytes 6291460
  7.2 33.1 %all-gather.4.cloned.1.call-start = ((), (), s32[]{:S(2)}) async-start(), calls=%async_computation.4 | async-start | bytes 1310720 | tf_op jit(solution)/shard_map/all_gather | solution.py:19
  7.9 74.4 %reduce-scatter.5.cloned.1.call-start = ((), (), s32[]{:S(2)}) async-start(), calls=%async_computation.5 | async-start | bytes 2621440 | tf_op jit(solution)/shard_map/reduce_scatter | solution.py:22
  47.6 63.7 %all-gather.6.cloned.1.call-start = ((), (), s32[]{:S(2)}) async-start(), calls=%async_computation.6 | async-start | bytes 1310720 | tf_op jit(solution)/shard_map/all_gather | solution.py:25
  84.1 30.0 %copy-start.4 = (s32[2,16]{1,0:T(2,128)S(1)}, s32[2,16]{1,0:T(2,128)}, u32[]{:S(2)}) copy-start(s32[2,16]{1,0:T(2,128)} %param.11) | copy-start | bytes 388
  84.2 51.9 %reduce-scatter.7.cloned.1.call-start = ((), (), s32[]{:S(2)}) async-start(), calls=%async_computation.7 | async-start | bytes 655360 | tf_op jit(solution)/shard_map/reduce_scatter | solution.py:26
  114.0 25.5 %copy-start.3 = (bf16[512,256]{1,0:T(8,128)(2,1)S(1)}, bf16[512,256]{1,0:T(8,128)(2,1)}, u32[]{:S(2)}) copy-start(bf16[512,256]{1,0:T(8,128)(2,1)} %param.7) | copy-start | bytes 786436
  114.1 155.5 %all-reduce.3.cloned.1.call-start = ((), (), s32[]{:S(2)}) async-start(), calls=%async_computation.8 | async-start | bytes 4194304 | tf_op jit(solution)/shard_map/psum | solution.py:41
  144.5 147.4 %all-reduce.5.cloned.1.call-start = ((), (), s32[]{:S(2)}) async-start(), calls=%async_computation.9 | async-start | bytes 524288 | tf_op jit(solution)/shard_map/psum | solution.py:42
  274.3 61.6 %reduce-scatter.9.cloned.1.call-start = ((), (), s32[]{:S(2)}) async-start(), calls=%async_computation.10 | async-start | bytes 1310720 | tf_op jit(solution)/shard_map/reduce_scatter | solution.py:52
  305.9 30.0 %copy-start.1 = (f32[2048,64]{0,1:T(8,128)S(1)}, f32[2048,64]{0,1:T(8,128)}, u32[]{:S(2)}) copy-start(f32[2048,64]{0,1:T(8,128)} %reduce-scatter.5.cloned.1.call-done) | copy-start | bytes 1572868
  307.7 57.2 %all-gather.8.cloned.1.call-start = ((), (), s32[]{:S(2)}) async-start(), calls=%async_computation.11 | async-start | bytes 1310720 | tf_op jit(solution)/shard_map/all_gather | solution.py:56
  337.6 34.3 %copy-start.2 = (bf16[512,256]{0,1:T(8,128)(2,1)S(1)}, bf16[512,256]{0,1:T(8,128)(2,1)}, u32[]{:S(2)}) copy-start(bf16[512,256]{0,1:T(8,128)(2,1)} %all-reduce.5.cloned.1.call-done) | copy-start | bytes 786436
  337.7 61.7 %reduce-scatter.11.cloned.1.call-start = ((), (), s32[]{:S(2)}) async-start(), calls=%async_computation.12 | async-start | bytes 1310720 | tf_op jit(solution)/shard_map/reduce_scatter | solution.py:57
Sparse Core Ops, SparseCore 0:
  9.6 30.6 all-gather.3
  47.7 34.5 reduce-scatter.4
  84.8 26.4 all-gather.5
  114.2 21.8 reduce-scatter.6
  144.6 124.8 all-reduce.2
  274.4 17.4 all-reduce.4
  307.8 28.0 reduce-scatter.8
  338.3 26.4 all-gather.7
  372.0 27.2 reduce-scatter.10
where the time goes:
time: 408 us
  waiting for transfers between devices  340 us (83%)
  matrix products  28.8 us (7%)
  blocking collectives  15.1 us (4%)
  between operations  14.6 us (4%)
  other arithmetic  6.41 us (2%)
    psum x1, waiting for transfers between devices, shards(): sep_mid = lax.psum(sep_part.astype(jnp.bfloat16), ('row', 'col'))  125 us
    reduce_scatter x1, waiting for transfers between devices, shards(): lax.psum_scatter(partial_value, 'row', scatter_dimension=1, tiled=True)  34.7 us
    all_gather x1, waiting for transfers between devices, shards(): lax.all_gather(sketch_leaf, 'col', axis=1, tiled=True)  32.3 us
    reduce_scatter x1, waiting for transfers between devices, shards(): lax.psum_scatter(back_part.astype(jnp.bfloat16), 'row', scatter_dimension...  28.2 us
    all_gather x1, waiting for transfers between devices, shards(): lax.all_gather(leaf_rhs, 'row', axis=1, tiled=True)  27.2 us
    all_gather x1, waiting for transfers between devices, shards(): lax.all_gather(front_z, 'row', axis=1, tiled=True)  27.1 us
    reduce_scatter x1, waiting for transfers between devices, shards(): lax.psum_scatter(out_part.astype(jnp.bfloat16), 'col', scatter_dimension=...  26.5 us
    reduce_scatter x1, waiting for transfers between devices, shards(): lax.psum_scatter(coupled_part, 'col', scatter_dimension=0, tiled=True)  21.7 us
  transfers between devices with their start and end apart: 9, of which 9 were waited for; matrix products, arithmetic and copies ran while one was open for 0% of the time, Pallas kernels for 0%

commit v1 on v0

--- a/solution.py
+++ b/solution.py
@@ -2,6 +2,27 @@
 import jax.numpy as jnp
 from jax import lax
 from jax.sharding import PartitionSpec as P
+
+
+def ring_gather(shard, axis, dim):
+    count, index, width = (lax.axis_size(axis), lax.axis_index(axis), shard.shape[dim])
+    forward = [(i, (i + 1) % count) for i in range(count)]
+    left = [(i, (i - 1) % count) for i in range(count)]
+    out = jnp.zeros((*shard.shape[:dim], count * width, *shard.shape[dim + 1 :]), shard.dtype)
+    out = lax.dynamic_update_slice_in_dim(out, shard, index * width, axis=dim)
+    from_left = from_right = shard
+    half = count // 2
+    for step in range(1, half + 1):
+        from_left = lax.ppermute(from_left, axis, forward)
+        out = lax.dynamic_update_slice_in_dim(
+            out, from_left, (index - step) % count * width, axis=dim
+        )
+        if step < count - half:
+            from_right = lax.ppermute(from_right, axis, left)
+            out = lax.dynamic_update_slice_in_dim(
+                out, from_right, (index + step) % count * width, axis=dim
+            )
+    return out
 
 
 def contract_rows(left, right):
@@ -15,9 +36,7 @@
     q_index = lax.axis_index("row") * lax.axis_size("col") + lax.axis_index("col")
     section = lax.axis_index("leaf")
     partial_value = jnp.dot(
-        leaf_inverse,
-        lax.all_gather(sketch_leaf, "col", axis=1, tiled=True),
-        preferred_element_type=jnp.float32,
+        leaf_inverse, ring_gather(sketch_leaf, "col", 1), preferred_element_type=jnp.float32
     )
     front_z = lax.psum_scatter(partial_value, "row", scatter_dimension=1, tiled=True).astype(
         jnp.bfloat16

time: 408 us -> 398 us (0.975)
  waiting for transfers between devices: 340 us -> 322 us
  starting transfers between devices: 0.37 us -> 5.53 us
    all_gather x1 -> x0, waiting for transfers between devices: 32.3 us -> none  [shards(): lax.all_gather(sketch_leaf, 'col', axis=1, tiled=True)]
    ppermute x0 -> x3, waiting for transfers between devices: none -> 15.6 us  [the longest x2 11.1 us: ring_gather(): from_left = lax.ppermute(from_left, axis, forward)]
    ppermute x0 -> x3, starting transfers between devices: none -> 5.2 us  [the longest x2 3.11 us: ring_gather(): from_left = lax.ppermute(from_left, axis, forward)]
  transfers between devices with their start and end apart: 9 -> 11, of which waited for: 9 -> 11; matrix products, arithmetic and copies ran while one was open for 0% -> 1% of each run, Pallas kernels for 0% -> 0%
where the time goes in v1:
time: 398 us
  waiting for transfers between devices  322 us (81%)
  matrix products  28.5 us (7%)
  blocking collectives  15.1 us (4%)
  between operations  15 us (4%)
  other arithmetic  6.41 us (2%)
  starting transfers between devices  5.53 us (1%)
  local copies, waits for them, and re-layouts  4.76 us (1%)
    psum x1, waiting for transfers between devices, shards(): sep_mid = lax.psum(sep_part.astype(jnp.bfloat16), ('row', 'col'))  125 us
    reduce_scatter x1, waiting for transfers between devices, shards(): lax.psum_scatter(partial_value, 'row', scatter_dimension=1, tiled=True)  34.7 us
    reduce_scatter x1, waiting for transfers between devices, shards(): lax.psum_scatter(back_part.astype(jnp.bfloat16), 'row', scatter_dimension...  28.2 us
    all_gather x1, waiting for transfers between devices, shards(): lax.all_gather(leaf_rhs, 'row', axis=1, tiled=True)  27.2 us
    all_gather x1, waiting for transfers between devices, shards(): lax.all_gather(front_z, 'row', axis=1, tiled=True)  27.1 us
    reduce_scatter x1, waiting for transfers between devices, shards(): lax.psum_scatter(out_part.astype(jnp.bfloat16), 'col', scatter_dimension=...  26.5 us
    reduce_scatter x1, waiting for transfers between devices, shards(): lax.psum_scatter(coupled_part, 'col', scatter_dimension=0, tiled=True)  21.7 us
    psum x1, waiting for transfers between devices, shards(): lax.psum(contract_rows(sep_inverse, sep_mid).astype(jnp.bfloat16), 'leaf')  16.3 us
  transfers between devices with their start and end apart: 11, of which 11 were waited for; matrix products, arithmetic and copies ran while one was open for 1% of the time, Pallas kernels for 0%

profile of v1, /device:TPU:0, one launch (start us, length us, event | category | flops | bytes accessed | tf_op | source)
XLA Modules:
  0.0 397.6 jit_solution(13191104217784781177)
XLA Ops:
  7.2 0.0 copy-start
  7.2 0.0 reduce-scatter.5.cloned.1.call-start
  7.2 3.1 collective-permute-start
  10.3 2.1 collective-permute-start.1
  12.4 0.1 broadcast_in_dim.2
  12.5 1.0 constant_dynamic-update-slice_fusion.3
  13.6 6.2 %collective-permute-done = bf16[2048,64]{0,1:T(8,128)(2,1)S(1)} collective-permute-done((bf16[2048,64]{0,1:T(8,128)(2,1)}, bf16[2048,64]{0,1:T(8,128)(2,1)S(1)}, u32[]{:S(2)}, u32[]{:S(2)}) %collective-permute-start) | collective-permute-done | bytes 262176 | tf_op jit(solution)/shard_map/ppermute | solution.py:16
  19.8 0.0 collective-permute-start.2
  19.8 4.5 %collective-permute-done.1 = bf16[2048,64]{0,1:T(8,128)(2,1)} collective-permute-done((bf16[2048,64]{0,1:T(8,128)(2,1)}, bf16[2048,64]{0,1:T(8,128)(2,1)}, u32[]{:S(2)}, u32[]{:S(2)}) %collective-permute-start.1) | collective-permute-done | bytes 262176 | tf_op jit(solution)/shard_map/ppermute | solution.py:21
  24.3 1.0 constant_dynamic-update-slice_fusion.1
  25.2 4.9 %collective-permute-done.2 = bf16[2048,64]{0,1:T(8,128)(2,1)S(1)} collective-permute-done((bf16[2048,64]{0,1:T(8,128)(2,1)S(1)}, bf16[2048,64]{0,1:T(8,128)(2,1)S(1)}, u32[]{:S(2)}, u32[]{:S(2)}) %collective-permute-start.2) | collective-permute-done | bytes 262176 | tf_op jit(solution)/shard_map/ppermute | solution.py:16
  30.2 7.1 %convolution_bitcast_fusion = f32[2048,256]{0,1:T(8,128)} fusion(bf16[2048,256]{0,1:T(8,128)(2,1)S(1)} %constant_dynamic-update-slice_fusion, bf16[2048,2048]{1,0:T(8,128)(2,1)} %param.8), kind=kOutput, calls=%fused_computation.2 | convolution fusion | flops 2147483648 | bytes 11534336 | tf_op jit(solution)/shard_map/dot_general | solution.py:38
  37.3 0.0 reduce-scatter.5.cloned.1.call-update
  37.3 0.0 all-gather.3.cloned.1.call-start
  37.3 34.7 %reduce-scatter.5.cloned.1.call-done = f32[2048,64]{0,1:T(8,128)} async-done(((f32[2048,256]{0,1:T(8,128)}), f32[2048,64]{0,1:T(8,128)}) %reduce-scatter.5.cloned.1.call-update) | async-done | bytes 524304 | tf_op jit(solution)/shard_map/reduce_scatter | solution.py:41
  72.0 1.8 convert_element_type.53
  73.8 0.0 all-gather.3.cloned.1.call-update
  73.8 0.0 copy-start.4
  73.8 0.0 reduce-scatter.7.cloned.1.call-start
  73.9 27.1 %all-gather.3.cloned.1.call-done = bf16[2048,256]{0,1:T(8,128)(2,1)} async-done(((bf16[2048,64]{0,1:T(8,128)(2,1)}), bf16[2048,256]{0,1:T(8,128)(2,1)}) %all-gather.3.cloned.1.call-update) | async-done | bytes 1048592 | tf_op jit(solution)/shard_map/all_gather | solution.py:44
  100.9 0.0 copy-done
  100.9 2.7 convolution_bitcast_fusion.1
  103.7 0.0 copy-start.3
  103.7 0.0 reduce-scatter.7.cloned.1.call-update
  103.7 0.0 all-reduce.3.cloned.1.call-start
  103.8 0.0 copy-done.4
  103.8 0.2 fusion.9
  103.9 21.7 %reduce-scatter.7.cloned.1.call-done = f32[128,256]{0,1:T(8,128)} async-done(((f32[512,256]{0,1:T(8,128)}), f32[128,256]{0,1:T(8,128)}) %reduce-scatter.7.cloned.1.call-update) | async-done | bytes 131088 | tf_op jit(solution)/shard_map/reduce_scatter | solution.py:45
  125.7 0.9 convert_element_type.56
  126.6 1.9 all_gather.13
  128.5 0.1 copy.10
  128.7 0.4 fusion.5
  129.1 0.1 copy.11
  129.2 0.0 copy-done.3
  129.2 0.1 fusion.4
  129.3 4.8 %fusion = bf16[4096,256]{0,1:T(8,128)(2,1)} fusion(bf16[512,256]{1,0:T(8,128)(2,1)S(1)} %fusion.4, bf16[4096,512]{1,0:T(8,128)(2,1)} %param.10), kind=kOutput, calls=%fused_computation.1 | convolution fusion | flops 1074790400 | bytes 6553600 | tf_op jit(solution)/shard_map/dot_general | solution.py:59
  134.1 0.0 all-reduce.3.cloned.1.call-update
  134.1 0.0 all-reduce.5.cloned.1.call-start
  134.2 125.0 %all-reduce.3.cloned.1.call-done = bf16[4096,256]{0,1:T(8,128)(2,1)} async-done(((bf16[4096,256]{0,1:T(8,128)(2,1)}), bf16[4096,256]{0,1:T(8,128)(2,1)}) %all-reduce.3.cloned.1.call-update) | async-done | bytes 2097168 | tf_op jit(solution)/shard_map/psum | solution.py:60
  259.2 4.8 %fusion.3 = bf16[512,256]{0,1:T(8,128)(2,1)} fusion(bf16[4096,256]{0,1:T(8,128)(2,1)} %all-reduce.3.cloned.1.call-done, bf16[4096,512]{1,0:T(8,128)(2,1)} %param.10), kind=kOutput, calls=%fused_computation.9 | convolution fusion | flops 1073872896 | bytes 6553600 | tf_op jit(solution)/shard_map/dot_general | solution.py:29
  263.9 0.0 all-reduce.5.cloned.1.call-update
  264.0 0.0 reduce-scatter.9.cloned.1.call-start
  264.0 0.6 dynamic_slice.10
  265.3 16.3 %all-reduce.5.cloned.1.call-done = bf16[512,256]{0,1:T(8,128)(2,1)} async-done(((bf16[512,256]{0,1:T(8,128)(2,1)}), bf16[512,256]{0,1:T(8,128)(2,1)}) %all-reduce.5.cloned.1.call-update) | async-done | bytes 262160 | tf_op jit(solution)/shard_map/psum | solution.py:61
  281.6 0.8 constant_dynamic-slice_fusion
  282.4 13.1 %all_gather.14 = bf16[512,256]{0,1:T(8,128)(2,1)S(1)} all-gather(bf16[128,256]{0,1:T(8,128)(2,1)S(1)} %constant_dynamic-slice_fusion), channel_id=1, replica_groups=mesh['leaf'=2,'row'=4,'col'=4] {'col'}, dimensions={0}, use_global_device_ids=true | all-gather | bytes 327680 | tf_op jit(solution)/shard_map/all_gather | solution.py:68
  295.6 0.0 copy-start.1
  295.6 1.7 fusion.2
  297.3 0.0 reduce-scatter.9.cloned.1.call-update
  297.3 0.0 all-gather.5.cloned.1.call-start
  297.3 28.2 %reduce-scatter.9.cloned.1.call-done = bf16[2048,64]{0,1:T(8,128)(2,1)} async-done(((bf16[2048,256]{0,1:T(8,128)(2,1)}), bf16[2048,64]{0,1:T(8,128)(2,1)}) %reduce-scatter.9.cloned.1.call-update) | async-done | bytes 262160 | tf_op jit(solution)/shard_map/reduce_scatter | solution.py:71
  325.5 0.0 copy-done.1
  325.6 1.7 subtract_convert_fusion
  327.2 0.0 all-gather.5.cloned.1.call-update
  327.3 0.0 copy-start.2
  327.3 0.0 reduce-scatter.11.cloned.1.call-start
  327.3 27.2 %all-gather.5.cloned.1.call-done = bf16[2048,256]{0,1:T(8,128)(2,1)} async-done(((bf16[2048,64]{0,1:T(8,128)(2,1)}), bf16[2048,256]{0,1:T(8,128)(2,1)}) %all-gather.5.cloned.1.call-update) | async-done | bytes 1048592 | tf_op jit(solution)/shard_map/all_gather | solution.py:75
  354.5 7.0 %fusion.1 = bf16[2048,256]{0,1:T(8,128)(2,1)} fusion(bf16[2048,256]{0,1:T(8,128)(2,1)} %all-gather.5.cloned.1.call-done, bf16[2048,2048]{1,0:T(8,128)(2,1)} %param.8), kind=kOutput, calls=%fused_computation.5 | convolution fusion | flops 2148007936 | bytes 10485760 | tf_op jit(solution)/shard_map/dot_general | solution.py:29
  361.5 0.0 reduce-scatter.11.cloned.1.call-update
  361.5 0.0 copy-done.2
  361.6 0.9 copy.12
  362.5 26.5 %reduce-scatter.11.cloned.1.call-done = bf16[2048,64]{0,1:T(8,128)(2,1)} async-done(((bf16[2048,256]{0,1:T(8,128)(2,1)}), bf16[2048,64]{0,1:T(8,128)(2,1)}) %reduce-scatter.11.cloned.1.call-update) | async-done | bytes 262160 | tf_op jit(solution)/shard_map/reduce_scatter | solution.py:76
  389.0 1.8 convert_element_type.68
  (3 shorter events, 0.1 us)
Async XLA Ops:
  7.2 93.8 %copy-start = (bf16[2048,512]{1,0:T(8,128)(2,1)S(1)}, bf16[2048,512]{1,0:T(8,128)(2,1)}, u32[]{:S(2)}) copy-start(bf16[2048,512]{1,0:T(8,128)(2,1)} %param.9) | copy-start | bytes 6291460
  7.2 64.8 %reduce-scatter.5.cloned.1.call-start = ((), (), s32[]{:S(2)}) async-start(), calls=%async_computation.4 | async-start | bytes 2621440 | tf_op jit(solution)/shard_map/reduce_scatter | solution.py:41
  7.2 12.5 %collective-permute-start = (bf16[2048,64]{0,1:T(8,128)(2,1)}, bf16[2048,64]{0,1:T(8,128)(2,1)S(1)}, u32[]{:S(2)}, u32[]{:S(2)}) collective-permute-start(bf16[2048,64]{0,1:T(8,128)(2,1)} %param.6), channel_id=1, source_target_pairs={{0,1},{1,2},{2,3},{3,0},{4,5},{5,6},{6,7},{7,4},{8,9},{9,10},{10,1... | collective-permute-start | bytes 786440 | tf_op jit(solution)/shard_map/ppermute | solution.py:16
  10.3 13.9 %collective-permute-start.1 = (bf16[2048,64]{0,1:T(8,128)(2,1)}, bf16[2048,64]{0,1:T(8,128)(2,1)}, u32[]{:S(2)}, u32[]{:S(2)}) collective-permute-start(bf16[2048,64]{0,1:T(8,128)(2,1)} %param.6), channel_id=1, source_target_pairs={{0,3},{1,0},{2,1},{3,2},{4,7},{5,4},{6,5},{7,6},{8,11},{9,8},{10,9... | collective-permute-start | bytes 786440 | tf_op jit(solution)/shard_map/ppermute | solution.py:21
  19.8 10.4 %collective-permute-start.2 = (bf16[2048,64]{0,1:T(8,128)(2,1)S(1)}, bf16[2048,64]{0,1:T(8,128)(2,1)S(1)}, u32[]{:S(2)}, u32[]{:S(2)}) collective-permute-start(bf16[2048,64]{0,1:T(8,128)(2,1)S(1)} %collective-permute-done), channel_id=1, source_target_pairs={{0,1},{1,2},{2,3},{3,0},{4,5},{5,6},{6,7},{7,4},{8,9},{9,10},{10,1... | collective-permute-start | bytes 786440 | tf_op jit(solution)/shard_map/ppermute | solution.py:16
  37.3 63.7 %all-gather.3.cloned.1.call-start = ((), (), s32[]{:S(2)}) async-start(), calls=%async_computation.5 | async-start | bytes 1310720 | tf_op jit(solution)/shard_map/all_gather | solution.py:44
  73.8 30.0 %copy-start.4 = (s32[2,16]{1,0:T(2,128)S(1)}, s32[2,16]{1,0:T(2,128)}, u32[]{:S(2)}) copy-start(s32[2,16]{1,0:T(2,128)} %param.11) | copy-start | bytes 388
  73.8 51.9 %reduce-scatter.7.cloned.1.call-start = ((), (), s32[]{:S(2)}) async-start(), calls=%async_computation.6 | async-start | bytes 655360 | tf_op jit(solution)/shard_map/reduce_scatter | solution.py:45
  103.7 25.5 %copy-start.3 = (bf16[512,256]{1,0:T(8,128)(2,1)S(1)}, bf16[512,256]{1,0:T(8,128)(2,1)}, u32[]{:S(2)}) copy-start(bf16[512,256]{1,0:T(8,128)(2,1)} %param.7) | copy-start | bytes 786436
  103.7 155.5 %all-reduce.3.cloned.1.call-start = ((), (), s32[]{:S(2)}) async-start(), calls=%async_computation.7 | async-start | bytes 4194304 | tf_op jit(solution)/shard_map/psum | solution.py:60
  134.1 147.4 %all-reduce.5.cloned.1.call-start = ((), (), s32[]{:S(2)}) async-start(), calls=%async_computation.8 | async-start | bytes 524288 | tf_op jit(solution)/shard_map/psum | solution.py:61
  264.0 61.6 %reduce-scatter.9.cloned.1.call-start = ((), (), s32[]{:S(2)}) async-start(), calls=%async_computation.9 | async-start | bytes 1310720 | tf_op jit(solution)/shard_map/reduce_scatter | solution.py:71
  295.6 30.0 %copy-start.1 = (f32[2048,64]{0,1:T(8,128)S(1)}, f32[2048,64]{0,1:T(8,128)}, u32[]{:S(2)}) copy-start(f32[2048,64]{0,1:T(8,128)} %reduce-scatter.5.cloned.1.call-done) | copy-start | bytes 1572868
  297.3 57.2 %all-gather.5.cloned.1.call-start = ((), (), s32[]{:S(2)}) async-start(), calls=%async_computation.10 | async-start | bytes 1310720 | tf_op jit(solution)/shard_map/all_gather | solution.py:75
  327.3 34.3 %copy-start.2 = (bf16[512,256]{0,1:T(8,128)(2,1)S(1)}, bf16[512,256]{0,1:T(8,128)(2,1)}, u32[]{:S(2)}) copy-start(bf16[512,256]{0,1:T(8,128)(2,1)} %all-reduce.5.cloned.1.call-done) | copy-start | bytes 786436
  327.3 61.7 %reduce-scatter.11.cloned.1.call-start = ((), (), s32[]{:S(2)}) async-start(), calls=%async_computation.11 | async-start | bytes 1310720 | tf_op jit(solution)/shard_map/reduce_scatter | solution.py:76
Sparse Core Ops, SparseCore 0:
  37.4 34.5 reduce-scatter.4
  74.4 26.4 all-gather.2
  103.8 21.8 reduce-scatter.6
  134.3 124.8 all-reduce.2
  264.1 17.4 all-reduce.4
  297.4 28.0 reduce-scatter.8
  328.0 26.4 all-gather.4
  361.7 27.2 reduce-scatter.10
